TPU v7x, 32 devices: a whole 2x2x4 slice. The times are simulated.
32 devices in a mesh: dp: 8 (over z, y), tp: 4 (over x, core).
Axes of the slice: x: 2, y: 2, z: 4, core: 2. Of those that a mesh axis runs over, the one named last changes fastest.
Arguments:
- hidden_in: bfloat16 [2, 8192, 1024], P(None, ('dp', 'tp')), may hold values from -6 to 6
- out_grad: bfloat16 [2, 8192, 1024], P(None, ('dp', 'tp')), may hold values from -6 to 6
- domain_ids: int32 [16], replicated, may hold values from 0 to 7
- domain_weights: float32 [8], replicated, may hold values from 0.5 to 2
- gain_attn: float32 [1024], P(('dp', 'tp')), may hold values from 0.1 to 1.9
- gain_mlp: float32 [1024], P(('dp', 'tp')), may hold values from 0.1 to 1.9
- w_query: bfloat16 [1024, 1024], P('dp', 'tp'), may hold values from -0.1875 to 0.1875
- w_kv: bfloat16 [1024, 256], P('dp', 'tp'), may hold values from -0.1875 to 0.1875
- w_out: bfloat16 [1024, 1024], P('tp', 'dp'), may hold values from -0.75 to 0.75
- w_gate: bfloat16 [1024, 2816], P('dp', 'tp'), may hold values from -0.1875 to 0.1875
- w_up: bfloat16 [1024, 2816], P('dp', 'tp'), may hold values from -0.1875 to 0.1875
- w_down: bfloat16 [2816, 1024], P('tp', 'dp'), may hold values from -0.109375 to 0.109375
Outputs:
- block_out: float32 [2, 8192, 1024], P(None, ('dp', 'tp'))
- input_grad: float32 [2, 8192, 1024], P(None, ('dp', 'tp'))
- gain_attn_grad: float32 [1024], P(('dp', 'tp'))
- gain_mlp_grad: float32 [1024], P(('dp', 'tp'))
- w_query_grad: float32 [1024, 1024], P('dp', 'tp')
- w_kv_grad: float32 [1024, 256], P('dp', 'tp')
- w_out_grad: float32 [1024, 1024], P('tp', 'dp')
- w_gate_grad: float32 [1024, 2816], P('dp', 'tp')
- w_up_grad: float32 [1024, 2816], P('dp', 'tp')
- w_down_grad: float32 [2816, 1024], P('tp', 'dp')
All inputs are finite; a program needn't handle non-finite values.
Results may differ from a plain program's by a relative error of at most 0.02.
Values may be sent and summed in bfloat16 or wider, within the bound.
No kernel may reach another device: no remote copies, remote signals or barrier semaphores. Data moves between devices by JAX's collectives and lax.ppermute only.
A program may use at most 192 MiB of HBM per device.

v0:
```python
import jax
import jax.numpy as jnp
from jax import lax
from jax.sharding import PartitionSpec as P

epsilon = 1e-06
neg_large = -1e30


def rope_tables(length, head_size):
    quarter = head_size // 4
    position = jnp.arange(length).astype(jnp.float32)
    frequency = 10000.0 ** (-jnp.arange(quarter).astype(jnp.float32) / quarter)
    angles = position[:, None] * frequency[None, :]
    return (jnp.cos(angles), jnp.sin(angles))


def rotate_half(values, cosine_table, sine_table):
    quarter = cosine_table.shape[-1]
    first_half = values[..., :quarter]
    paired = values[..., quarter : 2 * quarter]
    remainder = values[..., 2 * quarter :]
    return jnp.concatenate(
        [
            first_half * cosine_table - paired * sine_table,
            paired * cosine_table + first_half * sine_table,
            remainder,
        ],
        -1,
    )


def norm_forward(values, scales):
    inverse = lax.rsqrt(jnp.mean(values * values, -1, keepdims=True) + epsilon)
    unit_rows = values * inverse
    return (inverse, unit_rows, unit_rows * scales)


def norm_backward(grad_rows, inverse, unit_rows, scales):
    scaled = grad_rows * scales
    return inverse * (scaled - unit_rows * jnp.mean(scaled * unit_rows, -1, keepdims=True))


def masked_scores(query_block, key_rows, row_start):
    scores = jnp.einsum("tha,ua->htu", query_block, key_rows, preferred_element_type=jnp.float32)
    row_pos = row_start + jnp.arange(query_block.shape[0])
    col_pos = jnp.arange(key_rows.shape[0])
    return jnp.where(col_pos[None, None, :] <= row_pos[None, :, None], scores, neg_large)


def attend_forward(rotated, key_rows, value_rows):
    length = rotated.shape[0]
    block_rows = min(512, length)
    outputs = []
    totals = []
    for row_start in range(0, length, block_rows):
        scores = masked_scores(rotated[row_start : row_start + block_rows], key_rows, row_start)
        row_peak = jnp.max(scores, -1, keepdims=True)
        log_total = row_peak + jnp.log(jnp.sum(jnp.exp(scores - row_peak), -1, keepdims=True))
        probs_low = jnp.exp(scores - log_total).astype(jnp.bfloat16)
        outputs.append(
            jnp.einsum("htu,ua->tha", probs_low, value_rows, preferred_element_type=jnp.float32)
        )
        totals.append(log_total)
    return (jnp.concatenate(outputs, 0), totals)


def attend_backward(rotated, key_rows, value_rows, grad_mixed, totals):
    length = rotated.shape[0]
    block_rows = min(512, length)
    query_grads = []
    key_grad = jnp.zeros(key_rows.shape, jnp.float32)
    value_grad = jnp.zeros(value_rows.shape, jnp.float32)
    for block_idx, row_start in enumerate(range(0, length, block_rows)):
        query_block = rotated[row_start : row_start + block_rows]
        scores = masked_scores(query_block, key_rows, row_start)
        probs = jnp.exp(scores - totals[block_idx])
        probs_low = probs.astype(jnp.bfloat16)
        grad_block = grad_mixed[row_start : row_start + block_rows]
        grad_probs = jnp.einsum(
            "tha,ua->htu", grad_block, value_rows, preferred_element_type=jnp.float32
        )
        inner = jnp.sum(probs * grad_probs, -1, keepdims=True)
        grad_scores = (probs * (grad_probs - inner)).astype(jnp.bfloat16)
        query_grads.append(
            jnp.einsum("htu,ua->tha", grad_scores, key_rows, preferred_element_type=jnp.float32)
        )
        key_grad = key_grad + jnp.einsum(
            "htu,tha->ua", grad_scores, query_block, preferred_element_type=jnp.float32
        )
        value_grad = value_grad + jnp.einsum(
            "htu,tha->ua", probs_low, grad_block, preferred_element_type=jnp.float32
        )
    return (jnp.concatenate(query_grads, 0), key_grad, value_grad)


def local(
    hidden_in,
    out_grad,
    domain_ids,
    domain_weights,
    gain_attn,
    gain_mlp,
    w_query,
    w_kv,
    w_out,
    w_gate,
    w_up,
    w_down,
):
    micro = hidden_in.shape[0]
    n_data = lax.axis_size("dp")
    n_seqs = domain_ids.shape[0]
    head_size = w_kv.shape[1]
    per_group = w_query.shape[1] // head_size
    head_scale = head_size ** (-0.5)
    labels = jnp.arange(domain_weights.shape[0], dtype=jnp.int32)
    one_hot = (domain_ids[:, None] == labels[None, :]).astype(jnp.float32)
    counts = jnp.sum(one_hot, 0)
    gain_one, gain_two = (
        lax.all_gather(gain_attn, ("dp", "tp"), axis=0, tiled=True),
        lax.all_gather(gain_mlp, ("dp", "tp"), axis=0, tiled=True),
    )
    length = hidden_in.shape[1] * lax.axis_size("tp")
    cosine_table, sine_table = rope_tables(length, head_size)
    cos_heads = cosine_table[:, None, :]
    sin_heads = sine_table[:, None, :]
    gain_grad_one = jnp.zeros(gain_one.shape, jnp.float32)
    gain_grad_two = jnp.zeros(gain_two.shape, jnp.float32)
    outputs = []
    input_grads = []
    grad_totals = None
    for micro_idx in range(micro):
        weights_now = (
            lax.all_gather(w_query, "dp", axis=0, tiled=True),
            lax.all_gather(w_kv, "dp", axis=0, tiled=True),
            lax.all_gather(w_out, "dp", axis=1, tiled=True),
            lax.all_gather(w_gate, "dp", axis=0, tiled=True),
            lax.all_gather(w_up, "dp", axis=0, tiled=True),
            lax.all_gather(w_down, "dp", axis=1, tiled=True),
        )
        query_full, kv_full, out_full, gate_full, up_full, down_full = weights_now
        tokens = hidden_in[micro_idx].astype(jnp.float32)
        seq_index = micro_idx * n_data + lax.axis_index("dp")
        domain = lax.dynamic_index_in_dim(domain_ids, seq_index, keepdims=False)
        domain_pick = (labels == domain).astype(jnp.float32)
        factor = jnp.sum(domain_pick * domain_weights) * lax.rsqrt(
            jnp.sum(domain_pick * counts) * counts.shape[0] / n_seqs
        )
        inverse_one, unit_one, normed_one = norm_forward(tokens, gain_one)
        whole_one = lax.all_gather(normed_one.astype(jnp.bfloat16), "tp", axis=0, tiled=True)
        queries = jnp.dot(whole_one, query_full, preferred_element_type=jnp.float32).reshape(
            length, per_group, head_size
        )
        rotated = (rotate_half(queries, cos_heads, sin_heads) * head_scale).astype(jnp.bfloat16)
        kv_state = jnp.dot(whole_one, kv_full, preferred_element_type=jnp.float32)
        key_rows = rotate_half(kv_state, cosine_table, sine_table).astype(jnp.bfloat16)
        value_rows = kv_state.astype(jnp.bfloat16)
        mixed_out, totals = attend_forward(rotated, key_rows, value_rows)
        mixed_low = mixed_out.astype(jnp.bfloat16).reshape(length, per_group * head_size)
        attn_sum = lax.psum_scatter(
            jnp.dot(mixed_low, out_full, preferred_element_type=jnp.float32).astype(jnp.bfloat16),
            "tp",
            scatter_dimension=0,
            tiled=True,
        ).astype(jnp.float32)
        residual = tokens + attn_sum
        inverse_two, unit_two, normed_two = norm_forward(residual, gain_two)
        whole_two = lax.all_gather(normed_two.astype(jnp.bfloat16), "tp", axis=0, tiled=True)
        gate_val = jnp.dot(whole_two, gate_full, preferred_element_type=jnp.float32)
        up_val = jnp.dot(whole_two, up_full, preferred_element_type=jnp.float32)
        sigmoid_val = jax.nn.sigmoid(gate_val)
        silu_val = gate_val * sigmoid_val
        hidden_low = (silu_val * up_val).astype(jnp.bfloat16)
        branch = lax.psum_scatter(
            jnp.dot(hidden_low, down_full, preferred_element_type=jnp.float32).astype(jnp.bfloat16),
            "tp",
            scatter_dimension=0,
            tiled=True,
        ).astype(jnp.float32)
        outputs.append(residual + branch)
        weights_later = (
            lax.all_gather(w_query, "dp", axis=0, tiled=True),
            lax.all_gather(w_kv, "dp", axis=0, tiled=True),
            lax.all_gather(w_out, "dp", axis=1, tiled=True),
            lax.all_gather(w_gate, "dp", axis=0, tiled=True),
            lax.all_gather(w_up, "dp", axis=0, tiled=True),
            lax.all_gather(w_down, "dp", axis=1, tiled=True),
        )
        query_back, kv_back, out_back, gate_back, up_back, down_back = weights_later
        grad_out = out_grad[micro_idx].astype(jnp.float32) * factor
        grad_rows = lax.all_gather(grad_out.astype(jnp.bfloat16), "tp", axis=0, tiled=True)
        grad_hidden = jnp.einsum(
            "td,fd->tf", grad_rows, down_back, preferred_element_type=jnp.float32
        )
        grad_gate = (
            grad_hidden * up_val * sigmoid_val * (1.0 + gate_val * (1.0 - sigmoid_val))
        ).astype(jnp.bfloat16)
        grad_up = (grad_hidden * silu_val).astype(jnp.bfloat16)
        down_grad = jnp.einsum(
            "tf,td->fd", hidden_low, grad_rows, preferred_element_type=jnp.float32
        )
        gate_grad = jnp.einsum(
            "td,tf->df", whole_two, grad_gate, preferred_element_type=jnp.float32
        )
        up_grad = jnp.einsum("td,tf->df", whole_two, grad_up, preferred_element_type=jnp.float32)
        normed_two_part = jnp.einsum(
            "tf,df->td", grad_gate, gate_back, preferred_element_type=jnp.float32
        ) + jnp.einsum("tf,df->td", grad_up, up_back, preferred_element_type=jnp.float32)
        grad_normed_two = lax.psum_scatter(
            normed_two_part.astype(jnp.bfloat16), "tp", scatter_dimension=0, tiled=True
        ).astype(jnp.float32)
        gain_grad_two = gain_grad_two + jnp.sum(grad_normed_two * unit_two, 0)
        grad_residual = grad_out + norm_backward(grad_normed_two, inverse_two, unit_two, gain_two)
        grad_attn = lax.all_gather(grad_residual.astype(jnp.bfloat16), "tp", axis=0, tiled=True)
        out_grad_part = jnp.einsum(
            "tq,td->qd", mixed_low, grad_attn, preferred_element_type=jnp.float32
        )
        grad_mixed = jnp.einsum(
            "td,qd->tq", grad_attn, out_back, preferred_element_type=jnp.float32
        )
        grad_mixed = grad_mixed.astype(jnp.bfloat16).reshape(length, per_group, head_size)
        grad_rotated, key_grad, value_grad = attend_backward(
            rotated, key_rows, value_rows, grad_mixed, totals
        )
        grad_query = (rotate_half(grad_rotated, cos_heads, -sin_heads) * head_scale).astype(
            jnp.bfloat16
        )
        grad_query = grad_query.reshape(length, per_group * head_size)
        grad_kv = (value_grad + rotate_half(key_grad, cosine_table, -sine_table)).astype(
            jnp.bfloat16
        )
        query_grad = jnp.einsum(
            "td,tq->dq", whole_one, grad_query, preferred_element_type=jnp.float32
        )
        kv_grad = jnp.einsum("td,tk->dk", whole_one, grad_kv, preferred_element_type=jnp.float32)
        normed_one_part = jnp.einsum(
            "tq,dq->td", grad_query, query_back, preferred_element_type=jnp.float32
        ) + jnp.einsum("tk,dk->td", grad_kv, kv_back, preferred_element_type=jnp.float32)
        grad_normed_one = lax.psum_scatter(
            normed_one_part.astype(jnp.bfloat16), "tp", scatter_dimension=0, tiled=True
        ).astype(jnp.float32)
        gain_grad_one = gain_grad_one + jnp.sum(grad_normed_one * unit_one, 0)
        input_grads.append(
            grad_residual + norm_backward(grad_normed_one, inverse_one, unit_one, gain_one)
        )
        grads_now = (query_grad, kv_grad, out_grad_part, gate_grad, up_grad, down_grad)
        if micro_idx == 0:
            grad_totals = grads_now
        else:
            grad_totals = tuple((total + grad for total, grad in zip(grad_totals, grads_now)))
    query_total, kv_total, out_total, gate_total, up_total, down_total = grad_totals
    final_grads = (
        lax.psum_scatter(query_total, "dp", scatter_dimension=0, tiled=True),
        lax.psum_scatter(kv_total, "dp", scatter_dimension=0, tiled=True),
        lax.psum_scatter(out_total, "dp", scatter_dimension=1, tiled=True),
        lax.psum_scatter(gate_total, "dp", scatter_dimension=0, tiled=True),
        lax.psum_scatter(up_total, "dp", scatter_dimension=0, tiled=True),
        lax.psum_scatter(down_total, "dp", scatter_dimension=1, tiled=True),
    )
    gain_one_shard, gain_two_shard = (
        lax.psum_scatter(gain_grad_one, ("dp", "tp"), scatter_dimension=0, tiled=True),
        lax.psum_scatter(gain_grad_two, ("dp", "tp"), scatter_dimension=0, tiled=True),
    )
    return (
        jnp.stack(outputs, 0),
        jnp.stack(input_grads, 0),
        gain_one_shard,
        gain_two_shard,
        final_grads[0],
        final_grads[1],
        final_grads[2],
        final_grads[3],
        final_grads[4],
        final_grads[5],
    )


def solution(mesh):
    return jax.shard_map(
        local,
        mesh=mesh,
        in_specs=(
            P(None, ("dp", "tp"), None),
            P(None, ("dp", "tp"), None),
            P(),
            P(),
            P(("dp", "tp")),
            P(("dp", "tp")),
            P("dp", "tp"),
            P("dp", "tp"),
            P("tp", "dp"),
            P("dp", "tp"),
            P("dp", "tp"),
            P("tp", "dp"),
        ),
        out_specs=(
            P(None, ("dp", "tp"), None),
            P(None, ("dp", "tp"), None),
            P(("dp", "tp")),
            P(("dp", "tp")),
            P("dp", "tp"),
            P("dp", "tp"),
            P("tp", "dp"),
            P("dp", "tp"),
            P("dp", "tp"),
            P("tp", "dp"),
        ),
        check_vma=False,
    )
```

profile of v0, /device:TPU:0, one launch (start us, length us, event | category | flops | bytes accessed | tf_op | source)
XLA Modules:
  0.0 1190.9 jit_solution(2056927915261358699)
XLA Ops:
  11.3 42.1 %all-reduce.5 = (f32[1024]{0:T(1024)S(1)}, f32[1024]{0:T(1024)S(1)}) all-reduce(f32[1024]{0:T(1024)S(1)} %dynamic-update-slice, f32[1024]{0:T(1024)S(1)} %dynamic-update-slice.1), channel_id=1, replica_groups=mesh['dp'=8,'tp'=4] {'dp','tp'}, use_global_device_ids=true, to_apply=%add | all-reduce | flops 2048 | bytes 16384
  56.7 26.1 %all_gather.68 = bf16[1024,64]{0,1:T(8,128)(2,1)S(1)} all-gather(bf16[128,64]{0,1:T(8,128)(2,1)S(1)} %copy-done.81), channel_id=1, replica_groups=mesh['dp'=8,'tp'=4] {'dp'}, dimensions={0}, use_global_device_ids=true | all-gather | bytes 147456 | tf_op jit(solution)/shard_map/all_gather | solution.py:136
  83.0 33.3 %all_gather.69 = bf16[1024,256]{1,0:T(8,128)(2,1)} all-gather(bf16[128,256]{1,0:T(8,128)(2,1)S(1)} %copy-done.67), channel_id=1, replica_groups=mesh['dp'=8,'tp'=4] {'dp'}, dimensions={0}, use_global_device_ids=true | all-gather | bytes 589824 | tf_op jit(solution)/shard_map/all_gather | solution.py:135
  116.4 28.1 %all_gather.70 = bf16[256,1024]{1,0:T(8,128)(2,1)} all-gather(bf16[256,128]{1,0:T(8,128)(2,1)S(1)} %copy-done.68), channel_id=1, replica_groups=mesh['dp'=8,'tp'=4] {'dp'}, dimensions={1}, use_global_device_ids=true | all-gather | bytes 589824 | tf_op jit(solution)/shard_map/all_gather | solution.py:137
  193.9 13.0 %reduce-scatter.15.cloned.1.call-done = bf16[256,1024]{1,0:T(8,128)(2,1)} async-done(((bf16[1024,1024]{1,0:T(8,128)(2,1)}), bf16[256,1024]{1,0:T(8,128)(2,1)}) %reduce-scatter.15.cloned.1.call-update) | async-done | bytes 524304 | tf_op jit(solution)/shard_map/reduce_scatter | solution.py:161
  206.9 34.6 %reduce-scatter.19.cloned.1.call-done = bf16[256,1024]{1,0:T(8,128)(2,1)} async-done(((bf16[1024,1024]{1,0:T(8,128)(2,1)}), bf16[256,1024]{1,0:T(8,128)(2,1)}) %reduce-scatter.19.cloned.1.call-update) | async-done | bytes 524304 | tf_op jit(solution)/shard_map/reduce_scatter | solution.py:161
  273.5 39.8 %all-gather.16.cloned.1.call-done = bf16[1024,704]{0,1:T(8,128)(2,1)} async-done(((bf16[128,704]{0,1:T(8,128)(2,1)}), bf16[1024,704]{0,1:T(8,128)(2,1)}) %all-gather.16.cloned.1.call-update) | async-done | bytes 1441808 | tf_op jit(solution)/shard_map/all_gather | solution.py:138
  318.6 38.1 %all-gather.20.cloned.1.call-done = bf16[704,1024]{1,0:T(8,128)(2,1)} async-done(((bf16[704,128]{1,0:T(8,128)(2,1)}), bf16[704,1024]{1,0:T(8,128)(2,1)}) %all-gather.20.cloned.1.call-update) | async-done | bytes 1441808 | tf_op jit(solution)/shard_map/all_gather | solution.py:140
  356.8 22.3 %all-gather.30.cloned.1.call-done = bf16[1024,1024]{1,0:T(8,128)(2,1)} async-done(((bf16[256,1024]{1,0:T(8,128)(2,1)}), bf16[1024,1024]{1,0:T(8,128)(2,1)}) %all-gather.30.cloned.1.call-update) | async-done | bytes 2097168 | tf_op jit(solution)/shard_map/all_gather | solution.py:192
  412.4 23.2 %all-gather.26.cloned.1.call-done = bf16[1024,1024]{1,0:T(8,128)(2,1)} async-done(((bf16[256,1024]{1,0:T(8,128)(2,1)}), bf16[1024,1024]{1,0:T(8,128)(2,1)}) %all-gather.26.cloned.1.call-update) | async-done | bytes 2097168 | tf_op jit(solution)/shard_map/all_gather | solution.py:192
  454.3 26.2 %reduce-scatter.23.cloned.1.call-done = bf16[256,1024]{1,0:T(8,128)(2,1)} async-done(((bf16[1024,1024]{1,0:T(8,128)(2,1)}), bf16[256,1024]{1,0:T(8,128)(2,1)}) %reduce-scatter.23.cloned.1.call-update) | async-done | bytes 524304 | tf_op jit(solution)/shard_map/reduce_scatter | solution.py:210
  483.2 31.3 %reduce-scatter.21.cloned.1.call-done = bf16[256,1024]{1,0:T(8,128)(2,1)} async-done(((bf16[1024,1024]{1,0:T(8,128)(2,1)}), bf16[256,1024]{1,0:T(8,128)(2,1)}) %reduce-scatter.21.cloned.1.call-update) | async-done | bytes 524304 | tf_op jit(solution)/shard_map/reduce_scatter | solution.py:175
  518.9 21.9 %all-gather.32.cloned.1.call-done = bf16[1024,1024]{1,0:T(8,128)(2,1)} async-done(((bf16[256,1024]{1,0:T(8,128)(2,1)}), bf16[1024,1024]{1,0:T(8,128)(2,1)}) %all-gather.32.cloned.1.call-update) | async-done | bytes 2097168 | tf_op jit(solution)/shard_map/all_gather | solution.py:215
  551.4 13.9 %all-gather.28.cloned.1.call-done = bf16[1024,1024]{1,0:T(8,128)(2,1)} async-done(((bf16[256,1024]{1,0:T(8,128)(2,1)}), bf16[1024,1024]{1,0:T(8,128)(2,1)}) %all-gather.28.cloned.1.call-update) | async-done | bytes 2097168 | tf_op jit(solution)/shard_map/all_gather | solution.py:215
  568.5 14.1 %fusion.9 = (f32[4,512]{1,0:T(4,128)S(1)}, f32[4,512]{1,0:T(4,128)S(1)}, f32[1024,512,4]{1,0,2:T(8,128)}) fusion(f32[1024,512,4]{1,0,2:T(8,128)} %copy-done.1, f32[4,512]{1,0:T(4,128)S(1)} %log_add_fusion.3, pred[512,1024]{0,1:T(8,128)(4,1)S(1)} %iota_compare_fusion.1, f32[1024,512,4]{1,0,2:T(8,128)} %fusion.99, f32[4,512]{1,0:T(4,128)S(1)} %log_add_fusion.1, ...), kind=kOutput, calls=%fused_computation.17 | convolution fusion | flops 285208576 | bytes 34504704 | tf_op jit(solution)/shard_map/tha,ua->htu/dot_general | solution.py:80
  582.6 14.7 %fusion.11 = (bf16[4,512,1024]{1,2,0:T(8,128)(2,1)}, bf16[4,512,1024]{1,2,0:T(8,128)(2,1)S(1)}) fusion(f32[1024,512,4]{1,0,2:T(8,128)} %get-tuple-element.108, f32[1024,512,4]{1,0,2:T(8,128)} %copy-done.1, f32[4,512]{1,0:T(4,128)S(1)} %get-tuple-element.26, f32[4,512]{1,0:T(4,128)S(1)} %log_add_fusion.3, pred[512,1024]{0,1:T(8,128)(4,1)S(1)} %iota_compare_fusion.1, ...), kind=kLoop, calls=%fused_computation.19 | loop fusion | flops 20971520 | bytes 42500096 | tf_op jit(solution)/shard_map/convert_element_type | solution.py:84
  623.3 14.8 %fusion.8 = (bf16[4,512,1024]{1,2,0:T(8,128)(2,1)S(1)}, bf16[4,512,1024]{1,2,0:T(8,128)(2,1)}) fusion(f32[1024,512,4]{1,0,2:T(8,128)} %get-tuple-element.107, f32[1024,512,4]{1,0,2:T(8,128)} %copy-done, f32[4,512]{1,0:T(4,128)S(1)} %get-tuple-element.28, f32[4,512]{1,0:T(4,128)S(1)} %log_add_fusion.2, pred[512,1024]{0,1:T(8,128)(4,1)S(1)} %iota_compare_fusion, ...), kind=kLoop, calls=%fused_computation.14 | loop fusion | flops 20971520 | bytes 42500096 | tf_op jit(solution)/shard_map/convert_element_type | solution.py:84
  723.0 39.5 %all-reduce.4 = (f32[1024]{0:T(1024)S(1)}, f32[1024]{0:T(1024)S(1)}) all-reduce(f32[1024]{0:T(1024)S(1)} %add.272, f32[1024]{0:T(1024)S(1)} %add.273), channel_id=10, replica_groups=mesh['dp'=8,'tp'=4] {'dp','tp'}, use_global_device_ids=true, to_apply=%region_35.36.clone | all-reduce | flops 2048 | bytes 16384
  771.9 59.8 %reduce-scatter.41.cloned.1.call-done = f32[704,128]{1,0:T(8,128)} async-done(((f32[704,1024]{1,0:T(8,128)}), f32[704,128]{1,0:T(8,128)}) %reduce-scatter.41.cloned.1.call-update) | async-done | bytes 360464 | tf_op jit(solution)/shard_map/reduce_scatter | solution.py:259
  831.7 76.1 %reduce-scatter.39.cloned.1.call-done = f32[128,704]{0,1:T(8,128)} async-done(((f32[1024,704]{0,1:T(8,128)}), f32[128,704]{0,1:T(8,128)}) %reduce-scatter.39.cloned.1.call-update) | async-done | bytes 360464 | tf_op jit(solution)/shard_map/reduce_scatter | solution.py:258
  907.8 76.1 %reduce-scatter.37.cloned.1.call-done = f32[128,704]{0,1:T(8,128)} async-done(((f32[1024,704]{0,1:T(8,128)}), f32[128,704]{0,1:T(8,128)}) %reduce-scatter.37.cloned.1.call-update) | async-done | bytes 360464 | tf_op jit(solution)/shard_map/reduce_scatter | solution.py:257
  983.9 65.0 %reduce-scatter.33.cloned.1.call-done = f32[128,64]{0,1:T(8,128)} async-done(((f32[1024,64]{0,1:T(8,128)}), f32[128,64]{0,1:T(8,128)}) %reduce-scatter.33.cloned.1.call-update) | async-done | bytes 32784 | tf_op jit(solution)/shard_map/reduce_scatter | solution.py:255
  1048.9 67.2 %reduce-scatter.35.cloned.1.call-done = f32[256,128]{1,0:T(8,128)} async-done(((f32[256,1024]{1,0:T(8,128)}), f32[256,128]{1,0:T(8,128)}) %reduce-scatter.35.cloned.1.call-update) | async-done | bytes 131088 | tf_op jit(solution)/shard_map/reduce_scatter | solution.py:256
  1116.0 67.0 %reduce-scatter.31.cloned.1.call-done = f32[128,256]{1,0:T(8,128)} async-done(((f32[1024,256]{1,0:T(8,128)}), f32[128,256]{1,0:T(8,128)}) %reduce-scatter.31.cloned.1.call-update) | async-done | bytes 131088 | tf_op jit(solution)/shard_map/reduce_scatter | solution.py:254
  (418 shorter events, 282.1 us)
Async XLA Ops:
  8.0 136.9 %all-gather.22.cloned.1.call-start = ((), (), s32[]{:S(2)}) async-start(), calls=%async_computation.21 | async-start | bytes 2621440 | tf_op jit(solution)/shard_map/all_gather | solution.py:151
  55.9 92.2 %all-gather.12.cloned.1.call-start = ((), (), s32[]{:S(2)}) async-start(), calls=%async_computation.14 | async-start | bytes 2621440 | tf_op jit(solution)/shard_map/all_gather | solution.py:151
  56.6 150.2 %reduce-scatter.15.cloned.1.call-start = ((), (), s32[]{:S(2)}) async-start(), calls=%async_computation.15 | async-start | bytes 2621440 | tf_op jit(solution)/shard_map/reduce_scatter | solution.py:161
  175.4 66.1 %reduce-scatter.19.cloned.1.call-start = ((), (), s32[]{:S(2)}) async-start(), calls=%async_computation.22 | async-start | bytes 2621440 | tf_op jit(solution)/shard_map/reduce_scatter | solution.py:161
  193.2 62.4 %all-gather.18.cloned.1.call-start = ((), (), s32[]{:S(2)}) async-start(), calls=%async_computation.18 | async-start | bytes 1622016 | tf_op jit(solution)/shard_map/all_gather | solution.py:139
  193.8 74.4 %all-gather.24.cloned.1.call-start = ((), (), s32[]{:S(2)}) async-start(), calls=%async_computation.23 | async-start | bytes 2621440 | tf_op jit(solution)/shard_map/all_gather | solution.py:169
  245.7 67.6 %all-gather.16.cloned.1.call-start = ((), (), s32[]{:S(2)}) async-start(), calls=%async_computation.17 | async-start | bytes 1622016 | tf_op jit(solution)/shard_map/all_gather | solution.py:138
  246.3 110.5 %all-gather.20.cloned.1.call-start = ((), (), s32[]{:S(2)}) async-start(), calls=%async_computation.19 | async-start | bytes 1622016 | tf_op jit(solution)/shard_map/all_gather | solution.py:140
  247.0 132.0 %all-gather.30.cloned.1.call-start = ((), (), s32[]{:S(2)}) async-start(), calls=%async_computation.29 | async-start | bytes 2621440 | tf_op jit(solution)/shard_map/all_gather | solution.py:192
  253.7 150.0 %all-gather.14.cloned.1.call-start = ((), (), s32[]{:S(2)}) async-start(), calls=%async_computation.16 | async-start | bytes 2621440 | tf_op jit(solution)/shard_map/all_gather | solution.py:169
  254.5 181.2 %all-gather.26.cloned.1.call-start = ((), (), s32[]{:S(2)}) async-start(), calls=%async_computation.25 | async-start | bytes 2621440 | tf_op jit(solution)/shard_map/all_gather | solution.py:192
  255.1 199.3 %reduce-scatter.27.cloned.1.call-start = ((), (), s32[]{:S(2)}) async-start(), calls=%async_computation.30 | async-start | bytes 2621440 | tf_op jit(solution)/shard_map/reduce_scatter | solution.py:210
  392.3 88.2 %reduce-scatter.23.cloned.1.call-start = ((), (), s32[]{:S(2)}) async-start(), calls=%async_computation.26 | async-start | bytes 2621440 | tf_op jit(solution)/shard_map/reduce_scatter | solution.py:210
  448.9 65.5 %reduce-scatter.21.cloned.1.call-start = ((), (), s32[]{:S(2)}) async-start(), calls=%async_computation.24 | async-start | bytes 2621440 | tf_op jit(solution)/shard_map/reduce_scatter | solution.py:175
  454.1 86.8 %all-gather.32.cloned.1.call-start = ((), (), s32[]{:S(2)}) async-start(), calls=%async_computation.31 | async-start | bytes 2621440 | tf_op jit(solution)/shard_map/all_gather | solution.py:215
  518.9 189.4 %reduce-scatter.29.cloned.1.call-start = ((), (), s32[]{:S(2)}) async-start(), calls=%async_computation.32 | async-start | bytes 2621440 | tf_op jit(solution)/shard_map/reduce_scatter | solution.py:240
  655.1 65.9 %reduce-scatter.25.cloned.1.call-start = ((), (), s32[]{:S(2)}) async-start(), calls=%async_computation.28 | async-start | bytes 2621440 | tf_op jit(solution)/shard_map/reduce_scatter | solution.py:240
  668.1 98.4 %reduce-scatter.17.cloned.1.call-start = ((), (), s32[]{:S(2)}) async-start(), calls=%async_computation.20 | async-start | bytes 2621440 | tf_op jit(solution)/shard_map/reduce_scatter | solution.py:175
  673.0 158.7 %reduce-scatter.41.cloned.1.call-start = ((), (), s32[]{:S(2)}) async-start(), calls=%async_computation.38 | async-start | bytes 3244032 | tf_op jit(solution)/shard_map/reduce_scatter | solution.py:259
  680.1 227.6 %reduce-scatter.39.cloned.1.call-start = ((), (), s32[]{:S(2)}) async-start(), calls=%async_computation.37 | async-start | bytes 3244032 | tf_op jit(solution)/shard_map/reduce_scatter | solution.py:258
  687.4 296.5 %reduce-scatter.37.cloned.1.call-start = ((), (), s32[]{:S(2)}) async-start(), calls=%async_computation.36 | async-start | bytes 3244032 | tf_op jit(solution)/shard_map/reduce_scatter | solution.py:257
  694.6 354.3 %reduce-scatter.33.cloned.1.call-start = ((), (), s32[]{:S(2)}) async-start(), calls=%async_computation.34 | async-start | bytes 294912 | tf_op jit(solution)/shard_map/reduce_scatter | solution.py:255
  699.0 417.0 %reduce-scatter.35.cloned.1.call-start = ((), (), s32[]{:S(2)}) async-start(), calls=%async_computation.35 | async-start | bytes 1179648 | tf_op jit(solution)/shard_map/reduce_scatter | solution.py:256
  703.5 479.5 %reduce-scatter.31.cloned.1.call-start = ((), (), s32[]{:S(2)}) async-start(), calls=%async_computation.33 | async-start | bytes 1179648 | tf_op jit(solution)/shard_map/reduce_scatter | solution.py:254
  (120 other events, 3226.4 us)
Sparse Core Ops, SparseCore 0:
  56.0 22.3 all-gather.21
  80.6 22.5 all-gather.11
  175.5 31.3 reduce-scatter.14
  210.0 31.4 reduce-scatter.18
  392.5 31.7 reduce-scatter.26
  449.1 31.3 reduce-scatter.22
  483.0 31.3 reduce-scatter.20
Sparse Core Ops, SparseCore 1:
  195.7 42.9 all-gather.17
  245.8 22.4 all-gather.23
  270.2 43.1 all-gather.15
  315.4 41.3 all-gather.19
  358.3 20.6 all-gather.29
  381.2 22.4 all-gather.13
  405.2 30.4 all-gather.25
  518.4 22.4 all-gather.31
  542.9 22.4 all-gather.27
  655.2 31.4 reduce-scatter.28
  689.6 31.4 reduce-scatter.24
  723.7 31.4 reduce-scatter.16
  759.2 72.4 reduce-scatter.40
  835.8 71.9 reduce-scatter.38
  911.9 71.9 reduce-scatter.36
  987.8 61.0 reduce-scatter.32
  1052.9 63.1 reduce-scatter.34
  1120.4 62.5 reduce-scatter.30
where the time goes:
time: 1200 us; the launch traced here: 1190 us
  waiting for transfers between devices  717 us (60%)
  matrix products  200 us (17%)
  blocking collectives  169 us (14%)
  other arithmetic  69.8 us (6%)
  between operations  20.6 us (2%)
  local copies, waits for them, and re-layouts  12.5 us (1%)
    unnamed x2, blocking collectives  81.5 us
    reduce_scatter x1, waiting for transfers between devices, local(): lax.psum_scatter(gate_total, 'dp', scatter_dimension=0, tiled=True)  76.1 us
    reduce_scatter x1, waiting for transfers between devices, local(): lax.psum_scatter(up_total, 'dp', scatter_dimension=0, tiled=True)  76.1 us
    reduce_scatter x1, waiting for transfers between devices, local(): lax.psum_scatter(out_total, 'dp', scatter_dimension=1, tiled=True)  67.2 us
    reduce_scatter x1, waiting for transfers between devices, local(): lax.psum_scatter(query_total, 'dp', scatter_dimension=0, tiled=True)  67 us
    reduce_scatter x1, waiting for transfers between devices, local(): lax.psum_scatter(kv_total, 'dp', scatter_dimension=0, tiled=True)  65 us
    reduce_scatter x1, waiting for transfers between devices, local(): lax.psum_scatter(down_total, 'dp', scatter_dimension=1, tiled=True)  59.8 us
    reduce_scatter x2, waiting for transfers between devices, local(): lax.psum_scatter(jnp.dot(mixed_low, out_full, preferred_element_type=jnp....  47.6 us
  transfers between devices with their start and end apart: 25, of which 19 were waited for; matrix products, arithmetic and copies ran while one was open for 13% of the time, Pallas kernels for 0%

commit v1 on v0

--- a/solution.py
+++ b/solution.py
@@ -137,7 +137,9 @@
             lax.all_gather(w_out, "dp", axis=1, tiled=True),
             lax.all_gather(w_gate, "dp", axis=0, tiled=True),
             lax.all_gather(w_up, "dp", axis=0, tiled=True),
-            lax.all_gather(w_down, "dp", axis=1, tiled=True),
+            jnp.concatenate(
+                lax.all_to_all(jnp.stack([w_down] * lax.axis_size("dp")), "dp", 0, 0), axis=1
+            ),
         )
         query_full, kv_full, out_full, gate_full, up_full, down_full = weights_now
         tokens = hidden_in[micro_idx].astype(jnp.float32)

time: 1200 us -> 1210 us (level)
  blocking collectives: 169 us -> 209 us
  waiting for transfers between devices: 717 us -> 684 us
    all_to_all x0 -> x1, blocking collectives: none -> 40.4 us  [local(): lax.all_to_all(jnp.stack([w_down] * lax.axis_size('dp')), 'dp', 0, 0)]
    reduce_scatter x2, waiting for transfers between devices: 26.2 us -> 0.04 us  [local(): lax.psum_scatter(normed_two_part.astype(jnp.bfloat16), 'tp', scatter_dime...]
  transfers between devices with their start and end apart: 25 -> 25, of which waited for: 19 -> 18; matrix products, arithmetic and copies ran while one was open for 13% -> 13% of each run, Pallas kernels for 0% -> 0%
where the time goes in v1:
time: 1210 us; the launch traced here: 1200 us
  waiting for transfers between devices  684 us (57%)
  blocking collectives  209 us (17%)
  matrix products  198 us (16%)
  other arithmetic  69.6 us (6%)
  between operations  20.6 us (2%)
  local copies, waits for them, and re-layouts  13 us (1%)
    unnamed x2, blocking collectives  81.5 us
    reduce_scatter x1, waiting for transfers between devices, local(): lax.psum_scatter(up_total, 'dp', scatter_dimension=0, tiled=True)  76 us
    reduce_scatter x1, waiting for transfers between devices, local(): lax.psum_scatter(gate_total, 'dp', scatter_dimension=0, tiled=True)  75.5 us
    reduce_scatter x1, waiting for transfers between devices, local(): lax.psum_scatter(out_total, 'dp', scatter_dimension=1, tiled=True)  67 us
    reduce_scatter x1, waiting for transfers between devices, local(): lax.psum_scatter(query_total, 'dp', scatter_dimension=0, tiled=True)  66.9 us
    reduce_scatter x1, waiting for transfers between devices, local(): lax.psum_scatter(kv_total, 'dp', scatter_dimension=0, tiled=True)  64.9 us
    reduce_scatter x1, waiting for transfers between devices, local(): lax.psum_scatter(down_total, 'dp', scatter_dimension=1, tiled=True)  59.8 us
    reduce_scatter x2, waiting for transfers between devices, local(): lax.psum_scatter(jnp.dot(mixed_low, out_full, preferred_element_type=jnp....  47.6 us
  transfers between devices with their start and end apart: 25, of which 18 were waited for; matrix products, arithmetic and copies ran while one was open for 13% of the time, Pallas kernels for 0%

profile of v1, /device:TPU:0, one launch (start us, length us, event | category | flops | bytes accessed | tf_op | source)
XLA Modules:
  0.0 1197.7 jit_solution(7135087157578745638)
XLA Ops:
  11.3 42.1 %all-reduce.5 = (f32[1024]{0:T(1024)S(1)}, f32[1024]{0:T(1024)S(1)}) all-reduce(f32[1024]{0:T(1024)S(1)} %dynamic-update-slice, f32[1024]{0:T(1024)S(1)} %dynamic-update-slice.1), channel_id=1, replica_groups=mesh['dp'=8,'tp'=4] {'dp','tp'}, use_global_device_ids=true, to_apply=%add | all-reduce | flops 2048 | bytes 16384
  56.7 26.1 %all_gather.66 = bf16[1024,64]{0,1:T(8,128)(2,1)S(1)} all-gather(bf16[128,64]{0,1:T(8,128)(2,1)S(1)} %copy-done.84), channel_id=1, replica_groups=mesh['dp'=8,'tp'=4] {'dp'}, dimensions={0}, use_global_device_ids=true | all-gather | bytes 147456 | tf_op jit(solution)/shard_map/all_gather | solution.py:136
  83.0 33.3 %all_gather.67 = bf16[1024,256]{1,0:T(8,128)(2,1)} all-gather(bf16[128,256]{1,0:T(8,128)(2,1)S(1)} %copy-done.70), channel_id=1, replica_groups=mesh['dp'=8,'tp'=4] {'dp'}, dimensions={0}, use_global_device_ids=true | all-gather | bytes 589824 | tf_op jit(solution)/shard_map/all_gather | solution.py:135
  116.4 28.1 %all_gather.68 = bf16[256,1024]{1,0:T(8,128)(2,1)} all-gather(bf16[256,128]{1,0:T(8,128)(2,1)S(1)} %copy-done.71), channel_id=1, replica_groups=mesh['dp'=8,'tp'=4] {'dp'}, dimensions={1}, use_global_device_ids=true | all-gather | bytes 589824 | tf_op jit(solution)/shard_map/all_gather | solution.py:137
  192.9 13.0 %reduce-scatter.15.cloned.1.call-done = bf16[256,1024]{1,0:T(8,128)(2,1)} async-done(((bf16[1024,1024]{1,0:T(8,128)(2,1)}), bf16[256,1024]{1,0:T(8,128)(2,1)}) %reduce-scatter.15.cloned.1.call-update) | async-done | bytes 524304 | tf_op jit(solution)/shard_map/reduce_scatter | solution.py:163
  205.9 34.6 %reduce-scatter.19.cloned.1.call-done = bf16[256,1024]{1,0:T(8,128)(2,1)} async-done(((bf16[1024,1024]{1,0:T(8,128)(2,1)}), bf16[256,1024]{1,0:T(8,128)(2,1)}) %reduce-scatter.19.cloned.1.call-update) | async-done | bytes 524304 | tf_op jit(solution)/shard_map/reduce_scatter | solution.py:163
  272.6 39.8 %all-gather.16.cloned.1.call-done = bf16[1024,704]{0,1:T(8,128)(2,1)} async-done(((bf16[128,704]{0,1:T(8,128)(2,1)}), bf16[1024,704]{0,1:T(8,128)(2,1)}) %all-gather.16.cloned.1.call-update) | async-done | bytes 1441808 | tf_op jit(solution)/shard_map/all_gather | solution.py:138
  317.7 38.1 %all-gather.26.cloned.1.call-done = bf16[704,1024]{1,0:T(8,128)(2,1)} async-done(((bf16[704,128]{1,0:T(8,128)(2,1)}), bf16[704,1024]{1,0:T(8,128)(2,1)}) %all-gather.26.cloned.1.call-update) | async-done | bytes 1441808 | tf_op jit(solution)/shard_map/all_gather | solution.py:190
  355.8 22.3 %all-gather.30.cloned.1.call-done = bf16[1024,1024]{1,0:T(8,128)(2,1)} async-done(((bf16[256,1024]{1,0:T(8,128)(2,1)}), bf16[1024,1024]{1,0:T(8,128)(2,1)}) %all-gather.30.cloned.1.call-update) | async-done | bytes 2097168 | tf_op jit(solution)/shard_map/all_gather | solution.py:194
  411.5 23.1 %all-gather.24.cloned.1.call-done = bf16[1024,1024]{1,0:T(8,128)(2,1)} async-done(((bf16[256,1024]{1,0:T(8,128)(2,1)}), bf16[1024,1024]{1,0:T(8,128)(2,1)}) %all-gather.24.cloned.1.call-update) | async-done | bytes 2097168 | tf_op jit(solution)/shard_map/all_gather | solution.py:194
  448.2 40.4 %all_to_all.6 = bf16[8,704,128]{2,1,0:T(8,128)(2,1)S(1)} all-to-all(bf16[8,704,128]{2,1,0:T(8,128)(2,1)S(1)} %stack.14), channel_id=1, replica_groups=mesh['dp'=8,'tp'=4] {'dp'}, dimensions={0} | all-to-all | bytes 2883584 | tf_op jit(solution)/shard_map/all_to_all | solution.py:141
  495.9 26.3 %reduce-scatter.21.cloned.1.call-done = bf16[256,1024]{1,0:T(8,128)(2,1)} async-done(((bf16[1024,1024]{1,0:T(8,128)(2,1)}), bf16[256,1024]{1,0:T(8,128)(2,1)}) %reduce-scatter.21.cloned.1.call-update) | async-done | bytes 524304 | tf_op jit(solution)/shard_map/reduce_scatter | solution.py:177
  526.7 21.9 %all-gather.32.cloned.1.call-done = bf16[1024,1024]{1,0:T(8,128)(2,1)} async-done(((bf16[256,1024]{1,0:T(8,128)(2,1)}), bf16[1024,1024]{1,0:T(8,128)(2,1)}) %all-gather.32.cloned.1.call-update) | async-done | bytes 2097168 | tf_op jit(solution)/shard_map/all_gather | solution.py:217
  559.2 13.9 %all-gather.28.cloned.1.call-done = bf16[1024,1024]{1,0:T(8,128)(2,1)} async-done(((bf16[256,1024]{1,0:T(8,128)(2,1)}), bf16[1024,1024]{1,0:T(8,128)(2,1)}) %all-gather.28.cloned.1.call-update) | async-done | bytes 2097168 | tf_op jit(solution)/shard_map/all_gather | solution.py:217
  576.3 14.1 %fusion.9 = (f32[4,512]{1,0:T(4,128)S(1)}, f32[4,512]{1,0:T(4,128)S(1)}, f32[1024,512,4]{1,0,2:T(8,128)}) fusion(f32[1024,512,4]{1,0,2:T(8,128)} %copy-done.1, f32[4,512]{1,0:T(4,128)S(1)} %log_add_fusion.3, pred[512,1024]{0,1:T(8,128)(4,1)S(1)} %iota_compare_fusion.1, f32[1024,512,4]{1,0,2:T(8,128)} %fusion.103, f32[4,512]{1,0:T(4,128)S(1)} %log_add_fusion.1, ...), kind=kOutput, calls=%fused_computation.17 | convolution fusion | flops 285208576 | bytes 34504704 | tf_op jit(solution)/shard_map/tha,ua->htu/dot_general | solution.py:80
  590.4 14.7 %fusion.11 = (bf16[4,512,1024]{1,2,0:T(8,128)(2,1)}, bf16[4,512,1024]{1,2,0:T(8,128)(2,1)S(1)}) fusion(f32[1024,512,4]{1,0,2:T(8,128)} %get-tuple-element.108, f32[1024,512,4]{1,0,2:T(8,128)} %copy-done.1, f32[4,512]{1,0:T(4,128)S(1)} %get-tuple-element.26, f32[4,512]{1,0:T(4,128)S(1)} %log_add_fusion.3, pred[512,1024]{0,1:T(8,128)(4,1)S(1)} %iota_compare_fusion.1, ...), kind=kLoop, calls=%fused_computation.19 | loop fusion | flops 20971520 | bytes 42500096 | tf_op jit(solution)/shard_map/convert_element_type | solution.py:84
  631.1 14.8 %fusion.8 = (bf16[4,512,1024]{1,2,0:T(8,128)(2,1)S(1)}, bf16[4,512,1024]{1,2,0:T(8,128)(2,1)}) fusion(f32[1024,512,4]{1,0,2:T(8,128)} %get-tuple-element.107, f32[1024,512,4]{1,0,2:T(8,128)} %copy-done, f32[4,512]{1,0:T(4,128)S(1)} %get-tuple-element.28, f32[4,512]{1,0:T(4,128)S(1)} %log_add_fusion.2, pred[512,1024]{0,1:T(8,128)(4,1)S(1)} %iota_compare_fusion, ...), kind=kLoop, calls=%fused_computation.14 | loop fusion | flops 20971520 | bytes 42500096 | tf_op jit(solution)/shard_map/convert_element_type | solution.py:84
  730.7 39.5 %all-reduce.4 = (f32[1024]{0:T(1024)S(1)}, f32[1024]{0:T(1024)S(1)}) all-reduce(f32[1024]{0:T(1024)S(1)} %add.272, f32[1024]{0:T(1024)S(1)} %add.273), channel_id=10, replica_groups=mesh['dp'=8,'tp'=4] {'dp','tp'}, use_global_device_ids=true, to_apply=%region_35.36.clone | all-reduce | flops 2048 | bytes 16384
  779.6 59.8 %reduce-scatter.41.cloned.1.call-done = f32[704,128]{1,0:T(8,128)} async-done(((f32[704,1024]{1,0:T(8,128)}), f32[704,128]{1,0:T(8,128)}) %reduce-scatter.41.cloned.1.call-update) | async-done | bytes 360464 | tf_op jit(solution)/shard_map/reduce_scatter | solution.py:261
  839.4 76.0 %reduce-scatter.39.cloned.1.call-done = f32[128,704]{0,1:T(8,128)} async-done(((f32[1024,704]{0,1:T(8,128)}), f32[128,704]{0,1:T(8,128)}) %reduce-scatter.39.cloned.1.call-update) | async-done | bytes 360464 | tf_op jit(solution)/shard_map/reduce_scatter | solution.py:260
  915.4 75.5 %reduce-scatter.37.cloned.1.call-done = f32[128,704]{0,1:T(8,128)} async-done(((f32[1024,704]{0,1:T(8,128)}), f32[128,704]{0,1:T(8,128)}) %reduce-scatter.37.cloned.1.call-update) | async-done | bytes 360464 | tf_op jit(solution)/shard_map/reduce_scatter | solution.py:259
  990.9 64.9 %reduce-scatter.33.cloned.1.call-done = f32[128,64]{0,1:T(8,128)} async-done(((f32[1024,64]{0,1:T(8,128)}), f32[128,64]{0,1:T(8,128)}) %reduce-scatter.33.cloned.1.call-update) | async-done | bytes 32784 | tf_op jit(solution)/shard_map/reduce_scatter | solution.py:257
  1055.8 67.0 %reduce-scatter.35.cloned.1.call-done = f32[256,128]{1,0:T(8,128)} async-done(((f32[256,1024]{1,0:T(8,128)}), f32[256,128]{1,0:T(8,128)}) %reduce-scatter.35.cloned.1.call-update) | async-done | bytes 131088 | tf_op jit(solution)/shard_map/reduce_scatter | solution.py:258
  1122.9 66.9 %reduce-scatter.31.cloned.1.call-done = f32[128,256]{1,0:T(8,128)} async-done(((f32[1024,256]{1,0:T(8,128)}), f32[128,256]{1,0:T(8,128)}) %reduce-scatter.31.cloned.1.call-update) | async-done | bytes 131088 | tf_op jit(solution)/shard_map/reduce_scatter | solution.py:256
  (426 shorter events, 280.7 us)
Async XLA Ops:
  8.0 136.8 %all-gather.20.cloned.1.call-start = ((), (), s32[]{:S(2)}) async-start(), calls=%async_computation.21 | async-start | bytes 2621440 | tf_op jit(solution)/shard_map/all_gather | solution.py:153
  55.9 92.2 %all-gather.12.cloned.1.call-start = ((), (), s32[]{:S(2)}) async-start(), calls=%async_computation.15 | async-start | bytes 2621440 | tf_op jit(solution)/shard_map/all_gather | solution.py:153
  56.6 149.3 %reduce-scatter.15.cloned.1.call-start = ((), (), s32[]{:S(2)}) async-start(), calls=%async_computation.16 | async-start | bytes 2621440 | tf_op jit(solution)/shard_map/reduce_scatter | solution.py:163
  174.5 66.1 %reduce-scatter.19.cloned.1.call-start = ((), (), s32[]{:S(2)}) async-start(), calls=%async_computation.22 | async-start | bytes 2621440 | tf_op jit(solution)/shard_map/reduce_scatter | solution.py:163
  192.3 62.3 %all-gather.18.cloned.1.call-start = ((), (), s32[]{:S(2)}) async-start(), calls=%async_computation.19 | async-start | bytes 1622016 | tf_op jit(solution)/shard_map/all_gather | solution.py:139
  192.9 74.4 %all-gather.22.cloned.1.call-start = ((), (), s32[]{:S(2)}) async-start(), calls=%async_computation.23 | async-start | bytes 2621440 | tf_op jit(solution)/shard_map/all_gather | solution.py:171
  244.8 67.6 %all-gather.16.cloned.1.call-start = ((), (), s32[]{:S(2)}) async-start(), calls=%async_computation.18 | async-start | bytes 1622016 | tf_op jit(solution)/shard_map/all_gather | solution.py:138
  245.3 110.5 %all-gather.26.cloned.1.call-start = ((), (), s32[]{:S(2)}) async-start(), calls=%async_computation.26 | async-start | bytes 1622016 | tf_op jit(solution)/shard_map/all_gather | solution.py:190
  246.1 132.0 %all-gather.30.cloned.1.call-start = ((), (), s32[]{:S(2)}) async-start(), calls=%async_computation.30 | async-start | bytes 2621440 | tf_op jit(solution)/shard_map/all_gather | solution.py:194
  252.7 150.0 %all-gather.14.cloned.1.call-start = ((), (), s32[]{:S(2)}) async-start(), calls=%async_computation.17 | async-start | bytes 2621440 | tf_op jit(solution)/shard_map/all_gather | solution.py:171
  253.4 181.2 %all-gather.24.cloned.1.call-start = ((), (), s32[]{:S(2)}) async-start(), calls=%async_computation.25 | async-start | bytes 2621440 | tf_op jit(solution)/shard_map/all_gather | solution.py:194
  254.0 239.2 %reduce-scatter.27.cloned.1.call-start = ((), (), s32[]{:S(2)}) async-start(), calls=%async_computation.31 | async-start | bytes 2621440 | tf_op jit(solution)/shard_map/reduce_scatter | solution.py:212
  391.4 101.8 %reduce-scatter.23.cloned.1.call-start = ((), (), s32[]{:S(2)}) async-start(), calls=%async_computation.27 | async-start | bytes 2621440 | tf_op jit(solution)/shard_map/reduce_scatter | solution.py:212
  447.9 74.3 %reduce-scatter.21.cloned.1.call-start = ((), (), s32[]{:S(2)}) async-start(), calls=%async_computation.24 | async-start | bytes 2621440 | tf_op jit(solution)/shard_map/reduce_scatter | solution.py:177
  492.9 55.7 %all-gather.32.cloned.1.call-start = ((), (), s32[]{:S(2)}) async-start(), calls=%async_computation.32 | async-start | bytes 2621440 | tf_op jit(solution)/shard_map/all_gather | solution.py:217
  526.6 189.3 %reduce-scatter.29.cloned.1.call-start = ((), (), s32[]{:S(2)}) async-start(), calls=%async_computation.33 | async-start | bytes 2621440 | tf_op jit(solution)/shard_map/reduce_scatter | solution.py:242
  662.9 65.9 %reduce-scatter.25.cloned.1.call-start = ((), (), s32[]{:S(2)}) async-start(), calls=%async_computation.29 | async-start | bytes 2621440 | tf_op jit(solution)/shard_map/reduce_scatter | solution.py:242
  675.9 98.3 %reduce-scatter.17.cloned.1.call-start = ((), (), s32[]{:S(2)}) async-start(), calls=%async_computation.20 | async-start | bytes 2621440 | tf_op jit(solution)/shard_map/reduce_scatter | solution.py:177
  680.7 158.7 %reduce-scatter.41.cloned.1.call-start = ((), (), s32[]{:S(2)}) async-start(), calls=%async_computation.39 | async-start | bytes 3244032 | tf_op jit(solution)/shard_map/reduce_scatter | solution.py:261
  687.9 227.5 %reduce-scatter.39.cloned.1.call-start = ((), (), s32[]{:S(2)}) async-start(), calls=%async_computation.38 | async-start | bytes 3244032 | tf_op jit(solution)/shard_map/reduce_scatter | solution.py:260
  695.2 295.8 %reduce-scatter.37.cloned.1.call-start = ((), (), s32[]{:S(2)}) async-start(), calls=%async_computation.37 | async-start | bytes 3244032 | tf_op jit(solution)/shard_map/reduce_scatter | solution.py:259
  702.4 353.5 %reduce-scatter.33.cloned.1.call-start = ((), (), s32[]{:S(2)}) async-start(), calls=%async_computation.35 | async-start | bytes 294912 | tf_op jit(solution)/shard_map/reduce_scatter | solution.py:257
  706.8 416.1 %reduce-scatter.35.cloned.1.call-start = ((), (), s32[]{:S(2)}) async-start(), calls=%async_computation.36 | async-start | bytes 1179648 | tf_op jit(solution)/shard_map/reduce_scatter | solution.py:258
  711.2 478.6 %reduce-scatter.31.cloned.1.call-start = ((), (), s32[]{:S(2)}) async-start(), calls=%async_computation.34 | async-start | bytes 1179648 | tf_op jit(solution)/shard_map/reduce_scatter | solution.py:256
  (123 other events, 3233.8 us)
Sparse Core Ops, SparseCore 0:
  56.0 22.3 all-gather.19
  80.6 22.5 all-gather.11
  174.6 31.3 reduce-scatter.14
  209.1 31.4 reduce-scatter.18
  391.6 31.6 reduce-scatter.26
  448.1 31.4 reduce-scatter.22
  493.0 29.1 reduce-scatter.20
Sparse Core Ops, SparseCore 1:
  194.8 42.9 all-gather.17
  244.8 22.4 all-gather.21
  269.2 43.1 all-gather.15
  314.5 41.3 all-gather.25
  357.4 20.6 all-gather.29
  380.3 22.4 all-gather.13
  404.3 30.3 all-gather.23
  526.2 22.4 all-gather.31
  550.7 22.4 all-gather.27
  663.0 31.4 reduce-scatter.28
  697.4 31.3 reduce-scatter.24
  731.5 31.5 reduce-scatter.16
  767.0 72.3 reduce-scatter.40
  843.5 71.8 reduce-scatter.38
  919.6 71.3 reduce-scatter.36
  994.8 61.0 reduce-scatter.32
  1059.8 63.0 reduce-scatter.34
  1127.3 62.5 reduce-scatter.30
